TPU v7x, 512 devices: a whole 4x8x8 slice. The times are simulated.
512 devices in a mesh: row: 8 (over x, core), col: 64 (over z, y).
Axes of the slice: x: 4, y: 8, z: 8, core: 2. Of those that a mesh axis runs over, the one named last changes fastest.
Arguments:
- src_latent: bfloat16 [32, 32768], P(None, 'row'), may hold values from -6 to 6
- tgt_latent: bfloat16 [32, 131072], P(None, 'col'), may hold values from -6 to 6
- g_start: float32 [131072], P('col'), may hold values from -1.5 to 1.5
- pairs: int32 [8, 64, 8, 2], P('row', 'col'), may hold values from 0 to 7, as said below
- counts: int32 [8, 64], P('row', 'col'), may hold values from 1 to 8, as said below
Outputs:
- f_new: float32 [32768], P('row')
- g_new: float32 [131072], P('col')
- bary: float32 [32, 32768], P(None, 'row')
Inputs may be any that keep to these rules, and one draw needn't show every extreme that they name: Within one device's 8 slots all pairs are distinct; entry 0 is below 8 and entry 1 below 4. Every source block and every target block appears among the live slots of some device. `counts`: some device has exactly 8 live slots in every draw.
All inputs are finite; a program needn't handle non-finite values.
Results may differ from a plain program's by a relative error of at most 0.0012.
Values sent between devices are 32-bit elements; how exact they have to be, the bound alone decides.
No kernel may reach another device: no remote copies, remote signals or barrier semaphores. Data moves between devices by JAX's collectives and lax.ppermute only.
A program may use at most 64 MiB of HBM per device.

v0:
```python
import jax
import jax.numpy as jnp
from jax import lax
from jax.sharding import PartitionSpec as P

BLOCK = 512
epsilon = 0.01
very_low = -1e30


def body(src_latent, tgt_latent, g_start, pairs, counts):
    src_len = src_latent.shape[1]
    tgt_len = tgt_latent.shape[1]
    width = src_latent.shape[0]
    rows_all = src_len * lax.axis_size("row")
    cols_all = tgt_len * lax.axis_size("col")
    sq_src = jnp.sum(jnp.square(src_latent.astype(jnp.float32)), axis=0)
    sq_tgt = jnp.sum(jnp.square(tgt_latent.astype(jnp.float32)), axis=0)
    slots = pairs[0, 0]
    count = counts[0, 0]

    def tile_score(p, row_pot, col_pot):
        s_off = slots[p, 0] * BLOCK
        t_off = slots[p, 1] * BLOCK
        xs = lax.dynamic_slice_in_dim(src_latent, s_off, BLOCK, 1)
        ys = lax.dynamic_slice_in_dim(tgt_latent, t_off, BLOCK, 1)
        cross = lax.dot_general(
            xs, ys, (((0,), (0,)), ((), ())), preferred_element_type=jnp.float32
        )
        sx = lax.dynamic_slice_in_dim(sq_src, s_off, BLOCK)
        sy = lax.dynamic_slice_in_dim(sq_tgt, t_off, BLOCK)
        cost = (sx[:, None] + sy[None, :] - 2.0 * cross) / width
        shifted = -cost
        if row_pot is not None:
            shifted = shifted + lax.dynamic_slice_in_dim(row_pot, s_off, BLOCK)[:, None]
        if col_pot is not None:
            shifted = shifted + lax.dynamic_slice_in_dim(col_pot, t_off, BLOCK)[None, :]
        return (shifted / epsilon, s_off, t_off, ys)

    def expand(vec, axis):
        return vec[:, None] if axis == 1 else vec[None, :]

    def local_peak(row_pot, col_pot, axis, length):

        def step(p, peak):
            score, s_off, t_off, _ = tile_score(p, row_pot, col_pot)
            off = s_off if axis == 1 else t_off
            old = lax.dynamic_slice_in_dim(peak, off, BLOCK)
            return lax.dynamic_update_slice_in_dim(
                peak, jnp.maximum(old, jnp.max(score, axis=axis)), off, 0
            )

        return lax.fori_loop(0, count, step, jnp.full((length,), very_low, jnp.float32))

    def local_total(row_pot, col_pot, axis, length, peak):

        def step(p, total):
            score, s_off, t_off, _ = tile_score(p, row_pot, col_pot)
            off = s_off if axis == 1 else t_off
            top = expand(lax.dynamic_slice_in_dim(peak, off, BLOCK), axis)
            old = lax.dynamic_slice_in_dim(total, off, BLOCK)
            return lax.dynamic_update_slice_in_dim(
                total, old + jnp.sum(jnp.exp(score - top), axis=axis), off, 0
            )

        return lax.fori_loop(0, count, step, jnp.zeros((length,), jnp.float32))

    peak_f = lax.pmax(local_peak(None, g_start, 1, src_len), "col")
    total_f = lax.psum(local_total(None, g_start, 1, src_len, peak_f), "col")
    f_new = -epsilon * jnp.log(1.0 * rows_all) - epsilon * (peak_f + jnp.log(total_f))
    peak_g = lax.pmax(local_peak(f_new, None, 0, tgt_len), "row")
    total_g = lax.psum(local_total(f_new, None, 0, tgt_len, peak_g), "row")
    g_new = -epsilon * jnp.log(1.0 * cols_all) - epsilon * (peak_g + jnp.log(total_g))
    peak_b = lax.pmax(local_peak(None, g_new, 1, src_len), "col")

    def accumulate(p, carry):
        numer, denom = carry
        score, s_off, t_off, ys = tile_score(p, None, g_new)
        top = lax.dynamic_slice_in_dim(peak_b, s_off, BLOCK)
        weight = jnp.exp(score - top[:, None]).astype(jnp.bfloat16)
        part = lax.dot_general(
            ys, weight, (((1,), (1,)), ((), ())), preferred_element_type=jnp.float32
        )
        old = lax.dynamic_slice_in_dim(numer, s_off, BLOCK, 1)
        numer = lax.dynamic_update_slice_in_dim(numer, old + part, s_off, 1)
        old_den = lax.dynamic_slice_in_dim(denom, s_off, BLOCK)
        denom = lax.dynamic_update_slice_in_dim(
            denom, old_den + jnp.sum(weight.astype(jnp.float32), axis=1), s_off, 0
        )
        return (numer, denom)

    init = (jnp.zeros((width, src_len), jnp.float32), jnp.zeros((src_len,), jnp.float32))
    numer, denom = lax.fori_loop(0, count, accumulate, init)
    numer, denom = lax.psum((numer, denom), "col")
    bary = numer / denom[None, :]
    return (f_new, g_new, bary)


def solution(mesh):
    in_specs = (
        P(None, "row"),
        P(None, "col"),
        P("col"),
        P("row", "col", None, None),
        P("row", "col"),
    )
    out_specs = (P("row"), P("col"), P(None, "row"))
    return jax.shard_map(body, mesh=mesh, in_specs=in_specs, out_specs=out_specs, check_vma=False)
```

profile of v0, /device:TPU:4, one launch (start us, length us, event | category | flops | bytes accessed | tf_op | source)
XLA Modules:
  0.0 1290.6 jit_solution(17436968615771430454)
XLA Ops:
  7.2 1.0 multiply_reduce_fusion.1
  8.2 1.1 multiply_reduce_fusion
  9.3 0.6 copy-done.1
  10.0 25.1 %while.62 = (s32[]{:T(128)}, f32[4096]{0:T(1024)S(1)}, s32[]{:T(128)}, s32[8,2]{0,1:T(2,128)S(1)}, f32[4096]{0:T(1024)S(1)}, /*index=5*/f32[2048]{0:T(1024)S(1)}...) while((s32[]{:T(128)}, f32[4096]{0:T(1024)S(1)}, ...), condition=%wide.region_4.0_spmd, body=%wide.region_2.0_spmd.sunk | while | flops 18874380 | bytes 92479 | solution.py:53
  10.7 0.7 constant_dynamic-slice_fusion.18
  14.2 0.7 constant_dynamic-slice_fusion.18
  17.6 0.7 constant_dynamic-slice_fusion.18
  21.1 0.7 constant_dynamic-slice_fusion.18
  24.6 0.7 constant_dynamic-slice_fusion.18
  28.1 0.7 constant_dynamic-slice_fusion.18
  31.6 0.7 constant_dynamic-slice_fusion.18
  35.1 274.0 %pmax.21 = f32[4096]{0:T(1024)S(1)} all-reduce(f32[4096]{0:T(1024)S(1)} %get-tuple-element.312), channel_id=1, replica_groups=mesh['row'=8,'col'=64] {'col'}, use_global_device_ids=true, to_apply=%region_5.0 | all-reduce | flops 4096 | bytes 32768 | tf_op jit(solution)/shard_map/pmax | solution.py:68
  309.0 26.3 %while.63 = (s32[]{:T(128)}, f32[4096]{0:T(1024)S(1)}, s32[]{:T(128)}, s32[8,2]{0,1:T(2,128)S(1)}, f32[4096]{0:T(1024)S(1)}, /*index=5*/f32[2048]{0:T(1024)S(1)}...) while((s32[]{:T(128)}, f32[4096]{0:T(1024)S(1)}, ...), condition=%wide.region_8.0_spmd, body=%wide.region_6.0_spmd.sunk | while | flops 19136524 | bytes 98635 | solution.py:66
  309.7 0.7 constant_dynamic-slice_fusion.19
  313.4 0.7 constant_dynamic-slice_fusion.19
  317.0 0.7 constant_dynamic-slice_fusion.19
  320.7 0.7 constant_dynamic-slice_fusion.19
  324.4 0.7 constant_dynamic-slice_fusion.19
  328.1 0.7 constant_dynamic-slice_fusion.19
  331.7 0.7 constant_dynamic-slice_fusion.19
  335.4 274.0 %psum.28 = f32[4096]{0:T(1024)S(1)} all-reduce(f32[4096]{0:T(1024)S(1)} %get-tuple-element.313), channel_id=1, replica_groups=mesh['row'=8,'col'=64] {'col'}, use_global_device_ids=true, to_apply=%region_9.0 | all-reduce | flops 4096 | bytes 32768 | tf_op jit(solution)/shard_map/psum | solution.py:69
  609.4 24.8 %while.64 = (s32[]{:T(128)}, f32[2048]{0:T(1024)S(1)}, s32[]{:T(128)}, s32[8,2]{0,1:T(2,128)S(1)}, f32[4096]{0:T(1024)S(1)}, /*index=5*/f32[2048]{0:T(1024)S(1)}...) while((s32[]{:T(128)}, f32[2048]{0:T(1024)S(1)}, ...), condition=%wide.region_12.0_spmd, body=%wide.region_10.0_spmd.sunk | while | flops 18874380 | bytes 92479 | solution.py:53
  610.0 0.6 constant_dynamic-slice_fusion.20
  634.1 10.3 pmax.22
  644.4 25.9 %while.65 = (s32[]{:T(128)}, f32[2048]{0:T(1024)S(1)}, s32[]{:T(128)}, s32[8,2]{0,1:T(2,128)S(1)}, f32[4096]{0:T(1024)S(1)}, /*index=5*/f32[2048]{0:T(1024)S(1)}...) while((s32[]{:T(128)}, f32[2048]{0:T(1024)S(1)}, ...), condition=%wide.region_16.0_spmd, body=%wide.region_14.0_spmd.sunk | while | flops 19136524 | bytes 98635 | solution.py:66
  670.4 10.3 psum.29
  680.7 24.8 %while.66 = (s32[]{:T(128)}, f32[4096]{0:T(1024)S(1)}, s32[]{:T(128)}, s32[8,2]{0,1:T(2,128)S(1)}, f32[4096]{0:T(1024)S(1)}, /*index=5*/f32[2048]{0:T(1024)S(1)}...) while((s32[]{:T(128)}, f32[4096]{0:T(1024)S(1)}, ...), condition=%wide.region_20.0_spmd, body=%wide.region_18.0_spmd.sunk | while | flops 18874380 | bytes 92479 | solution.py:53
  705.5 274.0 %pmax.23 = f32[4096]{0:T(1024)S(1)} all-reduce(f32[4096]{0:T(1024)S(1)} %get-tuple-element.316), channel_id=1, replica_groups=mesh['row'=8,'col'=64] {'col'}, use_global_device_ids=true, to_apply=%region_21.0 | all-reduce | flops 4096 | bytes 32768 | tf_op jit(solution)/shard_map/pmax | solution.py:74
  979.5 27.4 %while.67 = (s32[]{:T(128)}, f32[32,4096]{1,0:T(8,128)S(1)}, f32[4096]{0:T(1024)S(1)}, s32[]{:T(128)}, s32[8,2]{0,1:T(2,128)S(1)}, /*index=5*/bf16[32,2048]{1,0:...) while((s32[]{:T(128)}, f32[32,4096]{1,0:T(8,128)S(1)}, ...), condition=%wide.region_24.0_spmd, body=%wide.region_22.0_spmd.sunk | while | flops 36454412 | bytes 1311067 | solution.py:93
  1007.0 0.8 copy-done
  1007.8 274.1 %psum.31 = f32[4096]{0:T(1024)S(1)} all-reduce(f32[4096]{0:T(1024)S(1)} %get-tuple-element.318), channel_id=1, replica_groups=mesh['row'=8,'col'=64] {'col'}, use_global_device_ids=true, to_apply=%region_26.0 | all-reduce | flops 4096 | bytes 32768 | tf_op jit(solution)/shard_map/psum | solution.py:94
  1281.9 1.9 broadcast_divide_fusion
  (289 shorter events, 58.2 us)
Async XLA Ops:
  7.2 2.2 copy-start.3
  7.2 1274.7 %all-reduce.2.cloned.1.call-start = ((), (), s32[]{:S(2)}) async-start(), calls=%async_computation | async-start | bytes 1048576 | tf_op jit(solution)/shard_map/psum | solution.py:94
  8.2 1.1 copy-start.2
  9.3 0.7 copy-start.1
  9.3 0.7 copy-start.6
  670.4 10.3 copy-start.5
  1006.9 0.8 copy-start
  1007.0 0.8 copy-start.4
Sparse Core Ops, SparseCore 0:
  1007.9 148.3 all-reduce.1
where the time goes:
time: 1290 us
  blocking collectives  1120 us (87%)
  loops' own time  86.6 us (7%)
  local copies, waits for them, and re-layouts  38.4 us (3%)
  matrix products  22.9 us (2%)
  between operations  14.2 us (1%)
    psum x1, blocking collectives, body(): numer, denom = lax.psum((numer, denom), 'col')  274 us
    pmax x1, blocking collectives, body(): peak_f = lax.pmax(local_peak(None, g_start, 1, src_len), 'col')  274 us
    psum x1, blocking collectives, body(): total_f = lax.psum(local_total(None, g_start, 1, src_len, peak_f), 'col')  274 us
    pmax x1, blocking collectives, body(): peak_b = lax.pmax(local_peak(None, g_new, 1, src_len), 'col')  274 us
    another operation x3, loops' own time, local_peak(): lax.fori_loop(0, count, step, jnp.full((length,), very_low, jnp.float32))  43.2 us
    another operation x2, loops' own time, local_total(): return lax.fori_loop(0, count, step, jnp.zeros((length,), jnp.float32))  28.8 us
  transfers between devices with their start and end apart: 1, of which 0 were waited for; matrix products, arithmetic and copies ran while one was open for 0% of the time, Pallas kernels for 0%

commit v1 on v0

--- a/solution.py
+++ b/solution.py
@@ -66,7 +66,7 @@
         return lax.fori_loop(0, count, step, jnp.zeros((length,), jnp.float32))
 
     peak_f = lax.pmax(local_peak(None, g_start, 1, src_len), "col")
-    total_f = lax.psum(local_total(None, g_start, 1, src_len, peak_f), "col")
+    total_f = jnp.sum(lax.all_gather(local_total(None, g_start, 1, src_len, peak_f), "col"), axis=0)
     f_new = -epsilon * jnp.log(1.0 * rows_all) - epsilon * (peak_f + jnp.log(total_f))
     peak_g = lax.pmax(local_peak(f_new, None, 0, tgt_len), "row")
     total_g = lax.psum(local_total(f_new, None, 0, tgt_len, peak_g), "row")

time: 1290 us -> 1100 us (0.85)
  blocking collectives: 1120 us -> 843 us
  waiting for transfers between devices: 0.02 us -> 76.8 us
    psum x1 -> x0, blocking collectives: 274 us -> none  [body(): total_f = lax.psum(local_total(None, g_start, 1, src_len, peak_f), 'col')]
    all_gather x0 -> x1, waiting for transfers between devices: none -> 76.7 us  [body(): lax.all_gather(local_total(None, g_start, 1, src_len, peak_f), 'col')]
  transfers between devices with their start and end apart: 1 -> 2, of which waited for: 0 -> 1; matrix products, arithmetic and copies ran while one was open for 0% -> 0% of each run, Pallas kernels for 0% -> 0%
where the time goes in v1:
time: 1100 us
  blocking collectives  843 us (77%)
  loops' own time  87.9 us (8%)
  waiting for transfers between devices  76.8 us (7%)
  local copies, waits for them, and re-layouts  40.7 us (4%)
  matrix products  22.7 us (2%)
  between operations  14.3 us (1%)
  other arithmetic  11.1 us (1%)
    psum x1, blocking collectives, body(): numer, denom = lax.psum((numer, denom), 'col')  274 us
    pmax x1, blocking collectives, body(): peak_f = lax.pmax(local_peak(None, g_start, 1, src_len), 'col')  274 us
    pmax x1, blocking collectives, body(): peak_b = lax.pmax(local_peak(None, g_new, 1, src_len), 'col')  274 us
    all_gather x1, waiting for transfers between devices, body(): lax.all_gather(local_total(None, g_start, 1, src_len, peak_f), 'col')  76.7 us
    another operation x3, loops' own time, local_peak(): lax.fori_loop(0, count, step, jnp.full((length,), very_low, jnp.float32))  44.2 us
    another operation x2, loops' own time, local_total(): return lax.fori_loop(0, count, step, jnp.zeros((length,), jnp.float32))  29.1 us
  transfers between devices with their start and end apart: 2, of which 1 were waited for; matrix products, arithmetic and copies ran while one was open for 0% of the time, Pallas kernels for 0%

profile of v1, /device:TPU:4, one launch (start us, length us, event | category | flops | bytes accessed | tf_op | source)
XLA Modules:
  0.0 1096.1 jit_solution(12165422128243809526)
XLA Ops:
  7.2 1.1 multiply_reduce_fusion
  8.4 0.6 copy-done.1
  9.1 25.7 %while.62 = (s32[]{:T(128)}, f32[4096]{0:T(1024)S(1)}, s32[]{:T(128)}, s32[8,2]{0,1:T(2,128)S(1)}, f32[4096]{0:T(1024)S(1)}, /*index=5*/f32[2048]{0:T(1024)S(1)}...) while((s32[]{:T(128)}, f32[4096]{0:T(1024)S(1)}, ...), condition=%wide.region_4.0_spmd, body=%wide.region_2.0_spmd.sunk | while | flops 18874380 | bytes 92471 | solution.py:53
  9.8 0.7 constant_dynamic-slice_fusion.18
  13.4 0.7 constant_dynamic-slice_fusion.18
  16.9 0.7 constant_dynamic-slice_fusion.18
  20.5 0.7 constant_dynamic-slice_fusion.18
  24.1 0.7 constant_dynamic-slice_fusion.18
  27.7 0.7 constant_dynamic-slice_fusion.18
  31.3 0.7 constant_dynamic-slice_fusion.18
  34.8 274.0 %pmax.21 = f32[4096]{0:T(1024)S(1)} all-reduce(f32[4096]{0:T(1024)S(1)} %get-tuple-element.312), channel_id=1, replica_groups=mesh['row'=8,'col'=64] {'col'}, use_global_device_ids=true, to_apply=%region_5.0 | all-reduce | flops 4096 | bytes 32768 | tf_op jit(solution)/shard_map/pmax | solution.py:68
  308.8 26.1 %while.63 = (s32[]{:T(128)}, f32[4096]{0:T(1024)S(1)}, s32[]{:T(128)}, s32[8,2]{0,1:T(2,128)S(1)}, f32[4096]{0:T(1024)S(1)}, /*index=5*/f32[2048]{0:T(1024)S(1)}...) while((s32[]{:T(128)}, f32[4096]{0:T(1024)S(1)}, ...), condition=%wide.region_8.0_spmd, body=%wide.region_6.0_spmd.sunk | while | flops 19136524 | bytes 98627 | solution.py:66
  335.0 0.6 copy-done.4
  335.6 76.7 %all-gather.3.cloned.1.call-done = f32[262144]{0:T(1024)} async-done(((f32[4096]{0:T(1024)}), f32[262144]{0:T(1024)}) %all-gather.3.cloned.1.call-update) | async-done | bytes 1048592 | tf_op jit(solution)/shard_map/all_gather | solution.py:69
  412.4 1.4 reshape.52
  413.9 25.6 %while.64 = (s32[]{:T(128)}, f32[2048]{0:T(1024)S(1)}, s32[]{:T(128)}, s32[8,2]{0,1:T(2,128)S(1)}, f32[4096]{0:T(1024)S(1)}, /*index=5*/f32[2048]{0:T(1024)S(1)}...) while((s32[]{:T(128)}, f32[2048]{0:T(1024)S(1)}, ...), condition=%wide.region_12.0_spmd, body=%wide.region_10.0_spmd.sunk | while | flops 18874380 | bytes 92471 | solution.py:53
  414.6 0.7 constant_dynamic-slice_fusion.20
  418.2 0.7 constant_dynamic-slice_fusion.20
  421.7 0.7 constant_dynamic-slice_fusion.20
  425.3 0.7 constant_dynamic-slice_fusion.20
  428.8 0.7 constant_dynamic-slice_fusion.20
  432.4 0.7 constant_dynamic-slice_fusion.20
  436.0 0.7 constant_dynamic-slice_fusion.20
  439.5 10.3 pmax.22
  449.8 26.0 %while.65 = (s32[]{:T(128)}, f32[2048]{0:T(1024)S(1)}, s32[]{:T(128)}, s32[8,2]{0,1:T(2,128)S(1)}, f32[4096]{0:T(1024)S(1)}, /*index=5*/f32[2048]{0:T(1024)S(1)}...) while((s32[]{:T(128)}, f32[2048]{0:T(1024)S(1)}, ...), condition=%wide.region_16.0_spmd, body=%wide.region_14.0_spmd.sunk | while | flops 19136524 | bytes 98627 | solution.py:66
  475.8 10.3 psum.21
  486.1 24.9 %while.66 = (s32[]{:T(128)}, f32[4096]{0:T(1024)S(1)}, s32[]{:T(128)}, s32[8,2]{0,1:T(2,128)S(1)}, f32[4096]{0:T(1024)S(1)}, /*index=5*/f32[2048]{0:T(1024)S(1)}...) while((s32[]{:T(128)}, f32[4096]{0:T(1024)S(1)}, ...), condition=%wide.region_20.0_spmd, body=%wide.region_18.0_spmd.sunk | while | flops 18874380 | bytes 92471 | solution.py:53
  510.9 274.0 %pmax.23 = f32[4096]{0:T(1024)S(1)} all-reduce(f32[4096]{0:T(1024)S(1)} %get-tuple-element.316), channel_id=1, replica_groups=mesh['row'=8,'col'=64] {'col'}, use_global_device_ids=true, to_apply=%region_21.0 | all-reduce | flops 4096 | bytes 32768 | tf_op jit(solution)/shard_map/pmax | solution.py:74
  784.9 27.5 %while.67 = (s32[]{:T(128)}, f32[32,4096]{1,0:T(8,128)S(1)}, f32[4096]{0:T(1024)S(1)}, s32[]{:T(128)}, s32[8,2]{0,1:T(2,128)S(1)}, /*index=5*/bf16[32,2048]{1,0:...) while((s32[]{:T(128)}, f32[32,4096]{1,0:T(8,128)S(1)}, ...), condition=%wide.region_24.0_spmd, body=%wide.region_22.0_spmd.sunk | while | flops 36454412 | bytes 1311059 | solution.py:93
  812.5 0.8 copy-done
  813.3 274.1 %psum.23 = f32[4096]{0:T(1024)S(1)} all-reduce(f32[4096]{0:T(1024)S(1)} %get-tuple-element.318), channel_id=1, replica_groups=mesh['row'=8,'col'=64] {'col'}, use_global_device_ids=true, to_apply=%region_26.0 | all-reduce | flops 4096 | bytes 32768 | tf_op jit(solution)/shard_map/psum | solution.py:94
  1087.4 1.9 broadcast_divide_fusion
  (295 shorter events, 58.8 us)
Async XLA Ops:
  7.2 405.2 %all-gather.3.cloned.1.call-start = ((), (), s32[]{:S(2)}) async-start(), calls=%async_computation.1 | async-start | bytes 1064960 | tf_op jit(solution)/shard_map/all_gather | solution.py:69
  7.2 1.1 copy-start.2
  7.2 1.2 copy-start.3
  8.4 0.7 copy-start.1
  8.4 0.7 copy-start.7
  335.0 0.6 copy-start.4
  335.6 751.8 %all-reduce.2.cloned.1.call-start = ((), (), s32[]{:S(2)}) async-start(), calls=%async_computation | async-start | bytes 1048576 | tf_op jit(solution)/shard_map/psum | solution.py:94
  475.8 10.3 copy-start.6
  812.4 0.8 copy-start
  812.5 0.8 copy-start.5
Sparse Core Ops, SparseCore 0:
  335.7 76.6 all-gather.2
  813.4 148.3 all-reduce.1
